TPU v7x, 512 devices: a whole 4x4x16 slice. The times are simulated.
512 devices in a mesh: slab: 128 (over x, z, y_hi), col: 4 (over y_lo, core).
Axes of the slice: x: 4, y: 4 (y_hi: 2, y_lo: 2; y = y_hi * 2 + y_lo), z: 16, core: 2. Of those that a mesh axis runs over, the one named last changes fastest.
Arguments:
- rhs: float32 [1024, 32, 384], P(('slab', 'col')), may hold values from -6 to 6
- tiles: bfloat16 [1024, 6, 384, 384], P(('slab', 'col'))
- neighbours: int32 [1024, 6], P(('slab', 'col')), may hold values from 0 to 1023, as said below
- smoother: bfloat16 [1024, 384, 384], P(('slab', 'col'))
- basis: bfloat16 [1024, 256, 384], P(('slab', 'col')), may hold values from -0.29882812 to 0.29882812
Outputs:
- solution: float32 [1024, 32, 384], P(('slab', 'col'))
- coarse_iterate: float32 [1024, 32, 256], P(('slab', 'col'))
Inputs may be any that keep to these rules, and one draw needn't show every extreme that they name: `neighbours`: entry [g, 0] is g itself; every other entry names a cell whose slab (cell // 8) is the slab of g or one of the two beside it, counted around 128 slabs.
All inputs are finite; a program needn't handle non-finite values.
Results may differ from a plain program's by a relative error of at most 0.0023.
The roundings to bfloat16 on the way count: a program that leaves them out, or rounds other values in their place, can miss the bound.
Values may be sent and summed in bfloat16 or wider, within the bound.
No kernel may reach another device: no remote copies, remote signals or barrier semaphores. Data moves between devices by JAX's collectives and lax.ppermute only.
A program may use at most 128 MiB of HBM per device.

v0:
```python
import jax
import jax.numpy as jnp
from jax import lax
from jax.sharding import PartitionSpec as P

damping = 0.8


def with_halo(cells, sides, width):
    for axis, dim in sides:
        count = lax.axis_size(axis)
        head = lax.slice_in_dim(cells, 0, width, axis=dim)
        tail = lax.slice_in_dim(cells, cells.shape[dim] - width, cells.shape[dim], axis=dim)
        cells = jnp.concatenate(
            [
                lax.ppermute(tail, axis, [(i, (i + 1) % count) for i in range(count)]),
                cells,
                lax.ppermute(head, axis, [((i + 1) % count, i) for i in range(count)]),
            ],
            axis=dim,
        )
    return cells


def neighbour_rows(vec_rounded):
    slab_rows = lax.all_gather(vec_rounded, "col", axis=0, tiled=True)
    return with_halo(slab_rows, (("slab", 0),), slab_rows.shape[0])


def per_device(rhs, tiles, neighbours, smoother, basis):
    cell_dev = rhs.shape[0]
    slab_count = lax.axis_size("slab")
    slab_cells = cell_dev * lax.axis_size("col")
    here = lax.axis_index("slab")
    slab_step = (neighbours // slab_cells - here + 1 + slab_count) % slab_count
    offset = neighbours % slab_cells
    row_place = slab_step * slab_cells + offset

    def smooth(residue):
        return jnp.einsum(
            "gri,gio->gro",
            residue.astype(jnp.bfloat16),
            smoother,
            preferred_element_type=jnp.float32,
        )

    def fine_apply(vec):
        near = neighbour_rows(vec.astype(jnp.bfloat16))
        picked = jnp.take(near, row_place, axis=0)
        return jnp.einsum("gtri,gtio->gro", picked, tiles, preferred_element_type=jnp.float32)

    x_first = smooth(rhs)
    x_second = x_first + smooth(rhs - fine_apply(x_first))
    fine_residual = rhs - fine_apply(x_second)
    wide_basis = lax.all_gather(basis, "col", axis=0, tiled=True)
    near_basis = with_halo(wide_basis, (("slab", 0),), wide_basis.shape[0])
    picked_basis = jnp.take(near_basis, row_place, axis=0)
    upper = jnp.einsum(
        "gtci,gtio->gtco", picked_basis, tiles, preferred_element_type=jnp.float32
    ).astype(jnp.bfloat16)
    coarse_tiles = jnp.einsum(
        "gtco,gdo->gtcd", upper, basis, preferred_element_type=jnp.float32
    ).astype(jnp.bfloat16)
    pivots = jnp.diagonal(coarse_tiles[:, 0].astype(jnp.float32), axis1=1, axis2=2)
    coarse_rhs = jnp.einsum(
        "gri,gci->grc",
        fine_residual.astype(jnp.bfloat16),
        basis,
        preferred_element_type=jnp.float32,
    )
    c_first = damping * coarse_rhs / pivots[:, None, :]
    near_coarse = neighbour_rows(c_first.astype(jnp.bfloat16))
    picked_coarse = jnp.take(near_coarse, row_place, axis=0)
    coarse_image = jnp.einsum(
        "gtrc,gtcd->grd", picked_coarse, coarse_tiles, preferred_element_type=jnp.float32
    )
    coarse_iterate = c_first + damping * (coarse_rhs - coarse_image) / pivots[:, None, :]
    solution = x_second + jnp.einsum(
        "grc,gci->gri",
        coarse_iterate.astype(jnp.bfloat16),
        basis,
        preferred_element_type=jnp.float32,
    )
    return (solution, coarse_iterate)


def solution(mesh):
    placed = (
        P(("slab", "col"), None, None),
        P(("slab", "col"), None, None, None),
        P(("slab", "col"), None),
        P(("slab", "col"), None, None),
        P(("slab", "col"), None, None),
    )
    return jax.shard_map(
        per_device,
        mesh=mesh,
        in_specs=placed,
        out_specs=(P(("slab", "col"), None, None), P(("slab", "col"), None, None)),
        check_vma=False,
    )
```

profile of v0, /device:TPU:1, one launch (start us, length us, event | category | flops | bytes accessed | tf_op | source)
XLA Modules:
  0.0 257.2 jit_solution(5884026762105295184)
XLA Ops:
  7.2 0.0 copy-start
  7.2 0.0 all-gather.2.cloned.1.call-start
  7.2 0.7 all-gather.2.cloned.1.call-update
  7.9 40.4 %all-gather.2.cloned.1.call-done = bf16[8,256,384]{2,1,0:T(8,128)(2,1)} async-done(((bf16[2,256,384]{2,1,0:T(8,128)(2,1)}), bf16[8,256,384]{2,1,0:T(8,128)(2,1)}) %all-gather.2.cloned.1.call-update) | async-done | bytes 1572880 | tf_op jit(solution)/shard_map/all_gather | solution.py:55
  48.3 9.9 %collective-permute-start.5 = (bf16[8,256,384]{2,1,0:T(8,128)(2,1)}, bf16[8,256,384]{2,1,0:T(8,128)(2,1)}, u32[]{:S(2)}, u32[]{:S(2)}) collective-permute-start(bf16[8,256,384]{2,1,0:T(8,128)(2,1)} %all-gather.2.cloned.1.call-done), channel_id=1, source_target_pairs={{4,0},{8,4},{12,8},{16,12},{20,16},{24,20},{28,24},{32,28},{36,32}... | collective-permute-start | bytes 4718600 | tf_op jit(solution)/shard_map/ppermute | solution.py:18
  58.2 1.9 collective-permute-start.4
  60.2 2.0 fusion.56
  62.1 62.8 %all_gather.12 = bf16[8,32,384]{2,1,0:T(8,128)(2,1)} all-gather(bf16[2,32,384]{2,1,0:T(8,128)(2,1)S(1)} %get-tuple-element.5), channel_id=1, replica_groups=mesh['slab'=128,'col'=4] {'col'}, dimensions={0}, use_global_device_ids=true | all-gather | bytes 245760 | tf_op jit(solution)/shard_map/all_gather | solution.py:26
  124.9 8.1 %collective-permute-start.1 = (bf16[8,32,384]{2,1,0:T(8,128)(2,1)}, bf16[8,32,384]{2,1,0:T(8,128)(2,1)}, u32[]{:S(2)}, u32[]{:S(2)}) collective-permute-start(bf16[8,32,384]{2,1,0:T(8,128)(2,1)} %all_gather.12), channel_id=1, source_target_pairs={{4,0},{8,4},{12,8},{16,12},{20,16},{24,20},{28,24},{32,28},{36,32}... | collective-permute-start | bytes 589832 | tf_op jit(solution)/shard_map/ppermute | solution.py:18
  132.9 1.9 collective-permute-start
  134.9 0.7 compare_and_fusion
  135.6 0.1 reshape.64
  135.7 1.7 collective-permute-done.1
  137.3 9.6 %collective-permute-done = bf16[8,32,384]{2,1,0:T(8,128)(2,1)} collective-permute-done((bf16[8,32,384]{2,1,0:T(8,128)(2,1)}, bf16[8,32,384]{2,1,0:T(8,128)(2,1)}, u32[]{:S(2)}, u32[]{:S(2)}) %collective-permute-start) | collective-permute-done | bytes 196640 | tf_op jit(solution)/shard_map/ppermute | solution.py:16
  146.9 2.0 pad_maximum_fusion.1
  148.9 2.4 gather_fusion.3
  151.3 0.0 copy-done
  151.3 2.7 %fusion.57 = (bf16[2,32,384]{2,1,0:T(8,128)(2,1)}, f32[2,32,384]{2,1,0:T(8,128)}) fusion(f32[2,32,384]{2,1,0:T(8,128)} %get-tuple-element.6, bf16[2,384,384]{2,1,0:T(8,128)(2,1)} %param.10, f32[2,32,384]{2,1,0:T(8,128)} %param.7, bf16[2,6,384,384]{3,2,1,0:T(8,128)(2,1)S(1)} %copy-done, bf16[2,6,32,384]{3,2,1,0:T(8,128)(2,1)} %bitcast.60, ...), kind=kOutput, calls=%fused_computation.67 | convolution fusion | flops 132366336 | bytes 4767756 | tf_op jit(solution)/shard_map/gri,gio->gro/dot_general | solution.py:40
  154.0 6.9 %all_gather.13 = bf16[8,32,384]{2,1,0:T(8,128)(2,1)S(1)} all-gather(bf16[2,32,384]{2,1,0:T(8,128)(2,1)} %get-tuple-element.7), channel_id=1, replica_groups=mesh['slab'=128,'col'=4] {'col'}, dimensions={0}, use_global_device_ids=true | all-gather | bytes 245760 | tf_op jit(solution)/shard_map/all_gather | solution.py:26
  160.9 4.2 %collective-permute-start.3 = (bf16[8,32,384]{2,1,0:T(8,128)(2,1)S(1)}, bf16[8,32,384]{2,1,0:T(8,128)(2,1)S(1)}, u32[]{:S(2)}, u32[]{:S(2)}) collective-permute-start(bf16[8,32,384]{2,1,0:T(8,128)(2,1)S(1)} %all_gather.13), channel_id=1, source_target_pairs={{4,0},{8,4},{12,8},{16,12},{20,16},{24,20},{28,24},{32,28},{36,32}... | collective-permute-start | bytes 589832 | tf_op jit(solution)/shard_map/ppermute | solution.py:18
  165.1 2.6 %collective-permute-start.2 = (bf16[8,32,384]{2,1,0:T(8,128)(2,1)S(1)}, bf16[8,32,384]{2,1,0:T(8,128)(2,1)S(1)}, u32[]{:S(2)}, u32[]{:S(2)}) collective-permute-start(bf16[8,32,384]{2,1,0:T(8,128)(2,1)S(1)} %all_gather.13), channel_id=1, source_target_pairs={{0,4},{4,8},{8,12},{12,16},{16,20},{20,24},{24,28},{28,32},{32,36}... | collective-permute-start | bytes 589832 | tf_op jit(solution)/shard_map/ppermute | solution.py:16
  167.7 2.9 %collective-permute-done.3 = bf16[8,32,384]{2,1,0:T(8,128)(2,1)S(1)} collective-permute-done((bf16[8,32,384]{2,1,0:T(8,128)(2,1)S(1)}, bf16[8,32,384]{2,1,0:T(8,128)(2,1)S(1)}, u32[]{:S(2)}, u32[]{:S(2)}) %collective-permute-start.3) | collective-permute-done | bytes 196640 | tf_op jit(solution)/shard_map/ppermute | solution.py:18
  170.6 8.2 %collective-permute-done.2 = bf16[8,32,384]{2,1,0:T(8,128)(2,1)S(1)} collective-permute-done((bf16[8,32,384]{2,1,0:T(8,128)(2,1)S(1)}, bf16[8,32,384]{2,1,0:T(8,128)(2,1)S(1)}, u32[]{:S(2)}, u32[]{:S(2)}) %collective-permute-start.2) | collective-permute-done | bytes 196640 | tf_op jit(solution)/shard_map/ppermute | solution.py:16
  178.8 0.9 pad_maximum_fusion.2
  179.6 2.4 gather_fusion.4
  182.0 0.0 collective-permute-done.5
  182.0 0.0 collective-permute-done.4
  182.0 4.2 %pad_maximum_fusion = bf16[24,256,384]{2,1,0:T(8,128)(2,1)} fusion(bf16[8,256,384]{2,1,0:T(8,128)(2,1)} %collective-permute-done.5, bf16[8,256,384]{2,1,0:T(8,128)(2,1)} %all-gather.2.cloned.1.call-done, bf16[8,256,384]{2,1,0:T(8,128)(2,1)} %collective-permute-done.4), kind=kLoop, calls=%fused_computation.5 | loop fusion | flops 4718592 | bytes 9437184 | tf_op jit(solution)/shard_map/concatenate | solution.py:14
  186.2 4.8 %gather_fusion = bf16[12,256,384]{2,1,0:T(8,128)(2,1)} fusion(bf16[24,256,384]{2,1,0:T(8,128)(2,1)} %pad_maximum_fusion, s32[1024]{0:T(1024)S(1)} %pad_clamp_fusion), kind=kCustom, calls=%fused_computation.2 | custom fusion | bytes 4718640 | tf_op jit(solution)/shard_map/jit(_take)/gather | solution.py:57
  191.0 5.3 %fusion.9 = bf16[2,6,256,256]{3,2,1,0:T(8,128)(2,1)} fusion(bf16[2,6,384,384]{3,2,1,0:T(8,128)(2,1)S(1)} %copy-done, bf16[2,6,256,384]{3,2,1,0:T(8,128)(2,1)} %bitcast.58, pred[2,6]{1,0:T(4,128)(4,1)S(1)} %get-tuple-element.3, bf16[2,256,384]{2,1,0:T(8,128)(2,1)} %param.11), kind=kOutput, calls=%fused_computation.11 | convolution fusion | flops 1513095168 | bytes 7864332 | tf_op jit(solution)/shard_map/gtco,gdo->gtcd/dot_general | solution.py:61
  196.3 1.8 fusion.34
  198.1 17.5 %copy.11 = f32[2,256,256]{0,2,1:T(8,128)} copy(f32[2,256,256]{2,1,0:T(8,128)} %fusion.34) | data formatting | bytes 1048576 | tf_op jit(solution)/shard_map/convert_element_type | solution.py:64
  215.6 3.0 %gather_fusion.1 = f32[256,2]{1,0:T(8,128)} fusion(f32[2,256,256]{0,2,1:T(8,128)} %copy.11, s32[256]{0:T(256)S(1)} %bitcast.57), kind=kCustom, calls=%fused_computation.3 | custom fusion | bytes 6144 | tf_op jit(solution)/shard_map/jit(diagonal)/gather | solution.py:64
  218.5 1.0 copy.12
  219.5 2.6 %fusion.42 = (bf16[2,32,256]{2,1,0:T(8,128)(2,1)}, f32[2,32,256]{2,1,0:T(8,128)}) fusion(f32[2,256]{1,0:T(2,128)S(1)} %copy.12, bf16[2,256,384]{2,1,0:T(8,128)(2,1)} %param.11, f32[2,32,384]{2,1,0:T(8,128)} %param.7, bf16[2,6,384,384]{3,2,1,0:T(8,128)(2,1)S(1)} %copy-done, bf16[2,6,32,384]{3,2,1,0:T(8,128)(2,1)} %bitcast.59, ...), kind=kOutput, calls=%fused_computation.43 | convolution fusion | flops 126074880 | bytes 4425740 | tf_op jit(solution)/shard_map/gri,gci->grc/dot_general | solution.py:65
  222.1 6.7 %all_gather.15 = bf16[8,32,256]{2,1,0:T(8,128)(2,1)S(1)} all-gather(bf16[2,32,256]{2,1,0:T(8,128)(2,1)} %get-tuple-element.9), channel_id=1, replica_groups=mesh['slab'=128,'col'=4] {'col'}, dimensions={0}, use_global_device_ids=true | all-gather | bytes 163840 | tf_op jit(solution)/shard_map/all_gather | solution.py:26
  228.9 2.5 collective-permute-start.7
  231.4 4.3 %collective-permute-start.6 = (bf16[8,32,256]{2,1,0:T(8,128)(2,1)S(1)}, bf16[8,32,256]{2,1,0:T(8,128)(2,1)S(1)}, u32[]{:S(2)}, u32[]{:S(2)}) collective-permute-start(bf16[8,32,256]{2,1,0:T(8,128)(2,1)S(1)} %all_gather.15), channel_id=1, source_target_pairs={{0,4},{4,8},{8,12},{12,16},{16,20},{20,24},{24,28},{28,32},{32,36}... | collective-permute-start | bytes 393224 | tf_op jit(solution)/shard_map/ppermute | solution.py:16
  235.7 1.5 collective-permute-done.7
  237.2 6.4 %collective-permute-done.6 = bf16[8,32,256]{2,1,0:T(8,128)(2,1)S(1)} collective-permute-done((bf16[8,32,256]{2,1,0:T(8,128)(2,1)S(1)}, bf16[8,32,256]{2,1,0:T(8,128)(2,1)S(1)}, u32[]{:S(2)}, u32[]{:S(2)}) %collective-permute-start.6) | collective-permute-done | bytes 131104 | tf_op jit(solution)/shard_map/ppermute | solution.py:16
  243.6 0.8 pad_maximum_fusion.3
  244.4 2.2 gather_fusion.2
  246.6 1.8 fusion.23
  248.4 0.0 copy-start.1
  248.5 1.9 convolution_add_fusion.1
  250.3 0.0 copy-done.1
  (2 shorter events, 0.0 us)
Async XLA Ops:
  7.2 144.1 %copy-start = (bf16[2,6,384,384]{3,2,1,0:T(8,128)(2,1)S(1)}, bf16[2,6,384,384]{3,2,1,0:T(8,128)(2,1)}, u32[]{:S(2)}) copy-start(bf16[2,6,384,384]{3,2,1,0:T(8,128)(2,1)} %param.8) | copy-start | bytes 10616836
  7.2 41.1 %all-gather.2.cloned.1.call-start = ((), (), s32[]{:S(2)}) async-start(), calls=%async_computation | async-start | bytes 1966080 | tf_op jit(solution)/shard_map/all_gather | solution.py:55
  48.3 133.8 %collective-permute-start.5 = (bf16[8,256,384]{2,1,0:T(8,128)(2,1)}, bf16[8,256,384]{2,1,0:T(8,128)(2,1)}, u32[]{:S(2)}, u32[]{:S(2)}) collective-permute-start(bf16[8,256,384]{2,1,0:T(8,128)(2,1)} %all-gather.2.cloned.1.call-done), channel_id=1, source_target_pairs={{4,0},{8,4},{12,8},{16,12},{20,16},{24,20},{28,24},{32,28},{36,32}... | collective-permute-start | bytes 4718600 | tf_op jit(solution)/shard_map/ppermute | solution.py:18
  58.2 123.8 %collective-permute-start.4 = (bf16[8,256,384]{2,1,0:T(8,128)(2,1)}, bf16[8,256,384]{2,1,0:T(8,128)(2,1)}, u32[]{:S(2)}, u32[]{:S(2)}) collective-permute-start(bf16[8,256,384]{2,1,0:T(8,128)(2,1)} %all-gather.2.cloned.1.call-done), channel_id=1, source_target_pairs={{0,4},{4,8},{8,12},{12,16},{16,20},{20,24},{24,28},{28,32},{32,36}... | collective-permute-start | bytes 4718600 | tf_op jit(solution)/shard_map/ppermute | solution.py:16
  124.9 12.5 %collective-permute-start.1 = (bf16[8,32,384]{2,1,0:T(8,128)(2,1)}, bf16[8,32,384]{2,1,0:T(8,128)(2,1)}, u32[]{:S(2)}, u32[]{:S(2)}) collective-permute-start(bf16[8,32,384]{2,1,0:T(8,128)(2,1)} %all_gather.12), channel_id=1, source_target_pairs={{4,0},{8,4},{12,8},{16,12},{20,16},{24,20},{28,24},{32,28},{36,32}... | collective-permute-start | bytes 589832 | tf_op jit(solution)/shard_map/ppermute | solution.py:18
  132.9 14.0 %collective-permute-start = (bf16[8,32,384]{2,1,0:T(8,128)(2,1)}, bf16[8,32,384]{2,1,0:T(8,128)(2,1)}, u32[]{:S(2)}, u32[]{:S(2)}) collective-permute-start(bf16[8,32,384]{2,1,0:T(8,128)(2,1)} %all_gather.12), channel_id=1, source_target_pairs={{0,4},{4,8},{8,12},{12,16},{16,20},{20,24},{24,28},{28,32},{32,36}... | collective-permute-start | bytes 589832 | tf_op jit(solution)/shard_map/ppermute | solution.py:16
  160.9 9.7 %collective-permute-start.3 = (bf16[8,32,384]{2,1,0:T(8,128)(2,1)S(1)}, bf16[8,32,384]{2,1,0:T(8,128)(2,1)S(1)}, u32[]{:S(2)}, u32[]{:S(2)}) collective-permute-start(bf16[8,32,384]{2,1,0:T(8,128)(2,1)S(1)} %all_gather.13), channel_id=1, source_target_pairs={{4,0},{8,4},{12,8},{16,12},{20,16},{24,20},{28,24},{32,28},{36,32}... | collective-permute-start | bytes 589832 | tf_op jit(solution)/shard_map/ppermute | solution.py:18
  165.1 13.6 %collective-permute-start.2 = (bf16[8,32,384]{2,1,0:T(8,128)(2,1)S(1)}, bf16[8,32,384]{2,1,0:T(8,128)(2,1)S(1)}, u32[]{:S(2)}, u32[]{:S(2)}) collective-permute-start(bf16[8,32,384]{2,1,0:T(8,128)(2,1)S(1)} %all_gather.13), channel_id=1, source_target_pairs={{0,4},{4,8},{8,12},{12,16},{16,20},{20,24},{24,28},{28,32},{32,36}... | collective-permute-start | bytes 589832 | tf_op jit(solution)/shard_map/ppermute | solution.py:16
  228.9 8.3 %collective-permute-start.7 = (bf16[8,32,256]{2,1,0:T(8,128)(2,1)S(1)}, bf16[8,32,256]{2,1,0:T(8,128)(2,1)S(1)}, u32[]{:S(2)}, u32[]{:S(2)}) collective-permute-start(bf16[8,32,256]{2,1,0:T(8,128)(2,1)S(1)} %all_gather.15), channel_id=1, source_target_pairs={{4,0},{8,4},{12,8},{16,12},{20,16},{24,20},{28,24},{32,28},{36,32}... | collective-permute-start | bytes 393224 | tf_op jit(solution)/shard_map/ppermute | solution.py:18
  231.4 12.2 %collective-permute-start.6 = (bf16[8,32,256]{2,1,0:T(8,128)(2,1)S(1)}, bf16[8,32,256]{2,1,0:T(8,128)(2,1)S(1)}, u32[]{:S(2)}, u32[]{:S(2)}) collective-permute-start(bf16[8,32,256]{2,1,0:T(8,128)(2,1)S(1)} %all_gather.15), channel_id=1, source_target_pairs={{0,4},{4,8},{8,12},{12,16},{16,20},{20,24},{24,28},{28,32},{32,36}... | collective-permute-start | bytes 393224 | tf_op jit(solution)/shard_map/ppermute | solution.py:16
  248.4 1.9 copy-start.1
Sparse Core Ops, SparseCore 0:
  10.1 38.1 all-gather.1
where the time goes:
time: 258 us; the launch traced here: 257 us
  blocking collectives  76.4 us (30%)
  waiting for transfers between devices  71.2 us (28%)
  starting transfers between devices  35.4 us (14%)
  local copies, waits for them, and re-layouts  33.3 us (13%)
  matrix products  16.3 us (6%)
  between operations  14.1 us (5%)
  other arithmetic  10.4 us (4%)
    all_gather x3, blocking collectives, neighbour_rows(): slab_rows = lax.all_gather(vec_rounded, 'col', axis=0, tiled=True)  76.4 us
    all_gather x1, waiting for transfers between devices, per_device(): wide_basis = lax.all_gather(basis, 'col', axis=0, tiled=True)  40.4 us
    ppermute x4, starting transfers between devices, with_halo(): lax.ppermute(head, axis, [((i + 1) % count, i) for i in range(count)])  24.7 us
    ppermute x4, waiting for transfers between devices, with_halo(): lax.ppermute(tail, axis, [(i, (i + 1) % count) for i in range(count)])  24.1 us
    convert_element_type x1, local copies, waits for them, and re-layouts, per_device(): coarse_tiles[:, 0].astype(jnp.float32)  17.5 us
    ppermute x4, starting transfers between devices, with_halo(): lax.ppermute(tail, axis, [(i, (i + 1) % count) for i in range(count)])  10.7 us
    concatenate x4, other arithmetic, with_halo(): jnp.concatenate([lax.ppermute(tail, axis, [(i, (i + 1) % count) for i in...  7.86 us
    ppermute x4, waiting for transfers between devices, with_halo(): lax.ppermute(head, axis, [((i + 1) % count, i) for i in range(count)])  6.03 us
  transfers between devices with their start and end apart: 9, of which 7 were waited for; matrix products, arithmetic and copies ran while one was open for 5% of the time, Pallas kernels for 0%

commit v1 on v0

--- a/solution.py
+++ b/solution.py
@@ -52,7 +52,10 @@
     x_first = smooth(rhs)
     x_second = x_first + smooth(rhs - fine_apply(x_first))
     fine_residual = rhs - fine_apply(x_second)
-    wide_basis = lax.all_gather(basis, "col", axis=0, tiled=True)
+    size = lax.axis_size("col")
+    blocks = jnp.stack([basis for _ in range(size)])
+    blocks = lax.all_to_all(blocks, "col", split_axis=0, concat_axis=0)
+    wide_basis = jnp.concatenate(blocks, axis=0)
     near_basis = with_halo(wide_basis, (("slab", 0),), wide_basis.shape[0])
     picked_basis = jnp.take(near_basis, row_place, axis=0)
     upper = jnp.einsum(

time: 258 us -> 235 us (0.911)
  waiting for transfers between devices: 71.2 us -> 30.7 us
  blocking collectives: 76.4 us -> 101 us
  between operations: 14.1 us -> 0.8 us
  starting transfers between devices: 35.4 us -> 41.4 us
    all_gather x1 -> x0, waiting for transfers between devices: 40.4 us -> none  [per_device(): wide_basis = lax.all_gather(basis, 'col', axis=0, tiled=True)]
    all_to_all x0 -> x1, blocking collectives: none -> 29.2 us  [per_device(): blocks = lax.all_to_all(blocks, 'col', split_axis=0, concat_axis=0)]
    ppermute x4, starting transfers between devices: 24.7 us -> 30.5 us  [with_halo(): lax.ppermute(head, axis, [((i + 1) % count, i) for i in range(count)])]
    all_gather x3, blocking collectives: 76.4 us -> 72 us  [neighbour_rows(): slab_rows = lax.all_gather(vec_rounded, 'col', axis=0, tiled=True)]
  transfers between devices with their start and end apart: 9 -> 8, of which waited for: 7 -> 6; matrix products, arithmetic and copies ran while one was open for 5% -> 5% of each run, Pallas kernels for 0% -> 0%
where the time goes in v1:
time: 235 us; the launch traced here: 233 us
  blocking collectives  101 us (43%)
  starting transfers between devices  41.4 us (18%)
  local copies, waits for them, and re-layouts  34.6 us (15%)
  waiting for transfers between devices  30.7 us (13%)
  matrix products  15.2 us (6%)
  other arithmetic  9.68 us (4%)
    all_gather x3, blocking collectives, neighbour_rows(): slab_rows = lax.all_gather(vec_rounded, 'col', axis=0, tiled=True)  72 us
    ppermute x4, starting transfers between devices, with_halo(): lax.ppermute(head, axis, [((i + 1) % count, i) for i in range(count)])  30.5 us
    all_to_all x1, blocking collectives, per_device(): blocks = lax.all_to_all(blocks, 'col', split_axis=0, concat_axis=0)  29.2 us
    ppermute x4, waiting for transfers between devices, with_halo(): lax.ppermute(tail, axis, [(i, (i + 1) % count) for i in range(count)])  24 us
    convert_element_type x1, local copies, waits for them, and re-layouts, per_device(): coarse_tiles[:, 0].astype(jnp.float32)  17.5 us
    ppermute x4, starting transfers between devices, with_halo(): lax.ppermute(tail, axis, [(i, (i + 1) % count) for i in range(count)])  10.9 us
    concatenate x4, other arithmetic, with_halo(): jnp.concatenate([lax.ppermute(tail, axis, [(i, (i + 1) % count) for i in...  7.86 us
    ppermute x4, waiting for transfers between devices, with_halo(): lax.ppermute(head, axis, [((i + 1) % count, i) for i in range(count)])  6.7 us
  transfers between devices with their start and end apart: 8, of which 6 were waited for; matrix products, arithmetic and copies ran while one was open for 5% of the time, Pallas kernels for 0%

profile of v1, /device:TPU:1, one launch (start us, length us, event | category | flops | bytes accessed | tf_op | source)
XLA Modules:
  0.0 233.5 jit_solution(5569991958105615460)
XLA Ops:
  0.6 0.0 copy-start
  0.6 0.0 copy-start.1
  0.7 0.0 copy-start.2
  0.7 1.3 stack.2
  2.0 0.0 copy-start.4
  2.0 29.2 %all_to_all.5 = bf16[4,2,256,384]{3,2,1,0:T(8,128)(2,1)} all-to-all(bf16[4,2,256,384]{3,2,1,0:T(8,128)(2,1)S(1)} %stack.2), channel_id=1, replica_groups=mesh['slab'=128,'col'=4] {'col'}, dimensions={0} | all-to-all | bytes 3145728 | tf_op jit(solution)/shard_map/all_to_all | solution.py:57
  31.1 10.6 %collective-permute-start.5 = (bf16[8,256,384]{2,1,0:T(8,128)(2,1)}, bf16[8,256,384]{2,1,0:T(8,128)(2,1)}, u32[]{:S(2)}, u32[]{:S(2)}) collective-permute-start(bf16[8,256,384]{2,1,0:T(8,128)(2,1)} %bitcast.6), channel_id=1, source_target_pairs={{4,0},{8,4},{12,8},{16,12},{20,16},{24,20},{28,24},{32,28},{36,32}... | collective-permute-start | bytes 4718600 | tf_op jit(solution)/shard_map/ppermute | solution.py:18
  41.7 1.9 collective-permute-start.4
  43.7 0.0 copy-done.1
  43.7 0.0 copy-done.2
  43.7 0.8 fusion.56
  44.5 58.3 %all_gather.9 = bf16[8,32,384]{2,1,0:T(8,128)(2,1)} all-gather(bf16[2,32,384]{2,1,0:T(8,128)(2,1)S(1)} %get-tuple-element.5), channel_id=1, replica_groups=mesh['slab'=128,'col'=4] {'col'}, dimensions={0}, use_global_device_ids=true | all-gather | bytes 245760 | tf_op jit(solution)/shard_map/all_gather | solution.py:26
  102.8 13.4 %collective-permute-start.1 = (bf16[8,32,384]{2,1,0:T(8,128)(2,1)}, bf16[8,32,384]{2,1,0:T(8,128)(2,1)}, u32[]{:S(2)}, u32[]{:S(2)}) collective-permute-start(bf16[8,32,384]{2,1,0:T(8,128)(2,1)} %all_gather.9), channel_id=1, source_target_pairs={{4,0},{8,4},{12,8},{16,12},{20,16},{24,20},{28,24},{32,28},{36,32}... | collective-permute-start | bytes 589832 | tf_op jit(solution)/shard_map/ppermute | solution.py:18
  116.2 1.9 collective-permute-start
  118.2 0.0 copy-done.4
  118.2 0.1 reshape.70
  118.3 2.3 collective-permute-done.1
  120.6 9.6 %collective-permute-done = bf16[8,32,384]{2,1,0:T(8,128)(2,1)} collective-permute-done((bf16[8,32,384]{2,1,0:T(8,128)(2,1)}, bf16[8,32,384]{2,1,0:T(8,128)(2,1)}, u32[]{:S(2)}, u32[]{:S(2)}) %collective-permute-start) | collective-permute-done | bytes 196640 | tf_op jit(solution)/shard_map/ppermute | solution.py:16
  130.2 2.0 pad_maximum_fusion.1
  132.2 2.4 %gather_fusion.3 = bf16[12,32,384]{2,1,0:T(8,128)(2,1)} fusion(bf16[24,32,384]{2,1,0:T(8,128)(2,1)} %pad_maximum_fusion.1, s32[1024]{0:T(1024)S(1)} %pad_clamp_fusion), kind=kCustom, calls=%fused_computation.clone | custom fusion | bytes 589872 | tf_op jit(solution)/shard_map/jit(_take)/gather | solution.py:49
  134.6 2.7 %fusion.57 = (bf16[2,32,384]{2,1,0:T(8,128)(2,1)}, f32[2,32,384]{2,1,0:T(8,128)}) fusion(f32[2,32,384]{2,1,0:T(8,128)} %get-tuple-element.6, bf16[2,384,384]{2,1,0:T(8,128)(2,1)} %param.10, f32[2,32,384]{2,1,0:T(8,128)} %param.7, bf16[2,6,384,384]{3,2,1,0:T(8,128)(2,1)S(1)} %copy-done, bf16[2,6,32,384]{3,2,1,0:T(8,128)(2,1)} %bitcast.61, ...), kind=kOutput, calls=%fused_computation.67 | convolution fusion | flops 132366336 | bytes 4767756 | tf_op jit(solution)/shard_map/gri,gio->gro/dot_general | solution.py:40
  137.3 6.9 %all_gather.10 = bf16[8,32,384]{2,1,0:T(8,128)(2,1)S(1)} all-gather(bf16[2,32,384]{2,1,0:T(8,128)(2,1)} %get-tuple-element.7), channel_id=1, replica_groups=mesh['slab'=128,'col'=4] {'col'}, dimensions={0}, use_global_device_ids=true | all-gather | bytes 245760 | tf_op jit(solution)/shard_map/all_gather | solution.py:26
  144.2 4.2 %collective-permute-start.3 = (bf16[8,32,384]{2,1,0:T(8,128)(2,1)S(1)}, bf16[8,32,384]{2,1,0:T(8,128)(2,1)S(1)}, u32[]{:S(2)}, u32[]{:S(2)}) collective-permute-start(bf16[8,32,384]{2,1,0:T(8,128)(2,1)S(1)} %all_gather.10), channel_id=1, source_target_pairs={{4,0},{8,4},{12,8},{16,12},{20,16},{24,20},{28,24},{32,28},{36,32}... | collective-permute-start | bytes 589832 | tf_op jit(solution)/shard_map/ppermute | solution.py:18
  148.4 2.6 %collective-permute-start.2 = (bf16[8,32,384]{2,1,0:T(8,128)(2,1)S(1)}, bf16[8,32,384]{2,1,0:T(8,128)(2,1)S(1)}, u32[]{:S(2)}, u32[]{:S(2)}) collective-permute-start(bf16[8,32,384]{2,1,0:T(8,128)(2,1)S(1)} %all_gather.10), channel_id=1, source_target_pairs={{0,4},{4,8},{8,12},{12,16},{16,20},{20,24},{24,28},{28,32},{32,36}... | collective-permute-start | bytes 589832 | tf_op jit(solution)/shard_map/ppermute | solution.py:16
  151.0 2.9 %collective-permute-done.3 = bf16[8,32,384]{2,1,0:T(8,128)(2,1)S(1)} collective-permute-done((bf16[8,32,384]{2,1,0:T(8,128)(2,1)S(1)}, bf16[8,32,384]{2,1,0:T(8,128)(2,1)S(1)}, u32[]{:S(2)}, u32[]{:S(2)}) %collective-permute-start.3) | collective-permute-done | bytes 196640 | tf_op jit(solution)/shard_map/ppermute | solution.py:18
  153.9 8.2 %collective-permute-done.2 = bf16[8,32,384]{2,1,0:T(8,128)(2,1)S(1)} collective-permute-done((bf16[8,32,384]{2,1,0:T(8,128)(2,1)S(1)}, bf16[8,32,384]{2,1,0:T(8,128)(2,1)S(1)}, u32[]{:S(2)}, u32[]{:S(2)}) %collective-permute-start.2) | collective-permute-done | bytes 196640 | tf_op jit(solution)/shard_map/ppermute | solution.py:16
  162.1 0.9 pad_maximum_fusion.2
  163.0 2.4 %gather_fusion.4 = bf16[12,32,384]{2,1,0:T(8,128)(2,1)} fusion(bf16[24,32,384]{2,1,0:T(8,128)(2,1)} %pad_maximum_fusion.2, s32[1024]{0:T(1024)S(1)} %pad_clamp_fusion), kind=kCustom, calls=%fused_computation.1.clone | custom fusion | bytes 589872 | tf_op jit(solution)/shard_map/jit(_take)/gather | solution.py:49
  165.3 0.0 collective-permute-done.5
  165.3 0.0 collective-permute-done.4
  165.3 4.2 %pad_maximum_fusion = bf16[24,256,384]{2,1,0:T(8,128)(2,1)} fusion(bf16[8,256,384]{2,1,0:T(8,128)(2,1)} %collective-permute-done.5, bf16[8,256,384]{2,1,0:T(8,128)(2,1)} %bitcast.6, bf16[8,256,384]{2,1,0:T(8,128)(2,1)} %collective-permute-done.4), kind=kLoop, calls=%fused_computation.5 | loop fusion | flops 4718592 | bytes 9437184 | tf_op jit(solution)/shard_map/concatenate | solution.py:14
  169.5 4.8 %gather_fusion = bf16[12,256,384]{2,1,0:T(8,128)(2,1)} fusion(bf16[24,256,384]{2,1,0:T(8,128)(2,1)} %pad_maximum_fusion, s32[1024]{0:T(1024)S(1)} %pad_clamp_fusion), kind=kCustom, calls=%fused_computation.2 | custom fusion | bytes 4718640 | tf_op jit(solution)/shard_map/jit(_take)/gather | solution.py:60
  174.3 5.3 %fusion.9 = bf16[2,6,256,256]{3,2,1,0:T(8,128)(2,1)} fusion(bf16[2,6,384,384]{3,2,1,0:T(8,128)(2,1)S(1)} %copy-done, bf16[2,6,256,384]{3,2,1,0:T(8,128)(2,1)} %bitcast.59, pred[2,6]{1,0:T(4,128)(4,1)S(1)} %get-tuple-element.3, bf16[2,256,384]{2,1,0:T(8,128)(2,1)} %param.11), kind=kOutput, calls=%fused_computation.11 | convolution fusion | flops 1513095168 | bytes 7864332 | tf_op jit(solution)/shard_map/gtco,gdo->gtcd/dot_general | solution.py:64
  179.6 1.8 fusion.34
  181.4 17.5 %copy.11 = f32[2,256,256]{0,2,1:T(8,128)} copy(f32[2,256,256]{2,1,0:T(8,128)} %fusion.34) | data formatting | bytes 1048576 | tf_op jit(solution)/shard_map/convert_element_type | solution.py:67
  198.9 3.0 %gather_fusion.1 = f32[256,2]{1,0:T(8,128)} fusion(f32[2,256,256]{0,2,1:T(8,128)} %copy.11, s32[256]{0:T(256)S(1)} %bitcast.58), kind=kCustom, calls=%fused_computation.3 | custom fusion | bytes 6144 | tf_op jit(solution)/shard_map/jit(diagonal)/gather | solution.py:67
  201.8 1.0 copy.12
  202.8 2.6 %fusion.42 = (bf16[2,32,256]{2,1,0:T(8,128)(2,1)}, f32[2,32,256]{2,1,0:T(8,128)}) fusion(f32[2,256]{1,0:T(2,128)S(1)} %copy.12, bf16[2,256,384]{2,1,0:T(8,128)(2,1)} %param.11, f32[2,32,384]{2,1,0:T(8,128)} %param.7, bf16[2,6,384,384]{3,2,1,0:T(8,128)(2,1)S(1)} %copy-done, bf16[2,6,32,384]{3,2,1,0:T(8,128)(2,1)} %bitcast.60, ...), kind=kOutput, calls=%fused_computation.43 | convolution fusion | flops 126074880 | bytes 4425740 | tf_op jit(solution)/shard_map/gri,gci->grc/dot_general | solution.py:68
  205.4 6.8 %all_gather.11 = bf16[8,32,256]{2,1,0:T(8,128)(2,1)S(1)} all-gather(bf16[2,32,256]{2,1,0:T(8,128)(2,1)} %get-tuple-element.9), channel_id=1, replica_groups=mesh['slab'=128,'col'=4] {'col'}, dimensions={0}, use_global_device_ids=true | all-gather | bytes 163840 | tf_op jit(solution)/shard_map/all_gather | solution.py:26
  212.2 2.3 collective-permute-start.7
  214.5 4.5 %collective-permute-start.6 = (bf16[8,32,256]{2,1,0:T(8,128)(2,1)S(1)}, bf16[8,32,256]{2,1,0:T(8,128)(2,1)S(1)}, u32[]{:S(2)}, u32[]{:S(2)}) collective-permute-start(bf16[8,32,256]{2,1,0:T(8,128)(2,1)S(1)} %all_gather.11), channel_id=1, source_target_pairs={{0,4},{4,8},{8,12},{12,16},{16,20},{20,24},{24,28},{28,32},{32,36}... | collective-permute-start | bytes 393224 | tf_op jit(solution)/shard_map/ppermute | solution.py:16
  219.0 1.5 collective-permute-done.7
  220.5 6.2 %collective-permute-done.6 = bf16[8,32,256]{2,1,0:T(8,128)(2,1)S(1)} collective-permute-done((bf16[8,32,256]{2,1,0:T(8,128)(2,1)S(1)}, bf16[8,32,256]{2,1,0:T(8,128)(2,1)S(1)}, u32[]{:S(2)}, u32[]{:S(2)}) %collective-permute-start.6) | collective-permute-done | bytes 131104 | tf_op jit(solution)/shard_map/ppermute | solution.py:16
  226.7 0.8 pad_maximum_fusion.3
  227.5 2.2 gather_fusion.2
  229.8 1.8 fusion.23
  231.6 0.0 copy-start.3
  231.6 1.9 convolution_add_fusion.1
  (5 shorter events, 0.0 us)
Async XLA Ops:
  0.6 134.0 %copy-start = (bf16[2,6,384,384]{3,2,1,0:T(8,128)(2,1)S(1)}, bf16[2,6,384,384]{3,2,1,0:T(8,128)(2,1)}, u32[]{:S(2)}) copy-start(bf16[2,6,384,384]{3,2,1,0:T(8,128)(2,1)} %param.8) | copy-start | bytes 10616836
  0.6 43.0 %copy-start.1 = (bf16[2,384,384]{2,1,0:T(8,128)(2,1)S(1)}, bf16[2,384,384]{2,1,0:T(8,128)(2,1)}, u32[]{:S(2)}) copy-start(bf16[2,384,384]{2,1,0:T(8,128)(2,1)} %param.10) | copy-start | bytes 1769476
  0.7 43.0 %copy-start.2 = (f32[2,32,384]{2,1,0:T(8,128)S(1)}, f32[2,32,384]{2,1,0:T(8,128)}, u32[]{:S(2)}) copy-start(f32[2,32,384]{2,1,0:T(8,128)} %param.7) | copy-start | bytes 294916
  2.0 116.2 %copy-start.4 = (s32[2,6]{1,0:T(2,128)S(1)}, s32[2,6]{1,0:T(2,128)}, u32[]{:S(2)}) copy-start(s32[2,6]{1,0:T(2,128)} %param.9) | copy-start | bytes 148
  31.1 134.2 %collective-permute-start.5 = (bf16[8,256,384]{2,1,0:T(8,128)(2,1)}, bf16[8,256,384]{2,1,0:T(8,128)(2,1)}, u32[]{:S(2)}, u32[]{:S(2)}) collective-permute-start(bf16[8,256,384]{2,1,0:T(8,128)(2,1)} %bitcast.6), channel_id=1, source_target_pairs={{4,0},{8,4},{12,8},{16,12},{20,16},{24,20},{28,24},{32,28},{36,32}... | collective-permute-start | bytes 4718600 | tf_op jit(solution)/shard_map/ppermute | solution.py:18
  41.7 123.6 %collective-permute-start.4 = (bf16[8,256,384]{2,1,0:T(8,128)(2,1)}, bf16[8,256,384]{2,1,0:T(8,128)(2,1)}, u32[]{:S(2)}, u32[]{:S(2)}) collective-permute-start(bf16[8,256,384]{2,1,0:T(8,128)(2,1)} %bitcast.6), channel_id=1, source_target_pairs={{0,4},{4,8},{8,12},{12,16},{16,20},{20,24},{24,28},{28,32},{32,36}... | collective-permute-start | bytes 4718600 | tf_op jit(solution)/shard_map/ppermute | solution.py:16
  102.8 17.8 %collective-permute-start.1 = (bf16[8,32,384]{2,1,0:T(8,128)(2,1)}, bf16[8,32,384]{2,1,0:T(8,128)(2,1)}, u32[]{:S(2)}, u32[]{:S(2)}) collective-permute-start(bf16[8,32,384]{2,1,0:T(8,128)(2,1)} %all_gather.9), channel_id=1, source_target_pairs={{4,0},{8,4},{12,8},{16,12},{20,16},{24,20},{28,24},{32,28},{36,32}... | collective-permute-start | bytes 589832 | tf_op jit(solution)/shard_map/ppermute | solution.py:18
  116.2 14.0 %collective-permute-start = (bf16[8,32,384]{2,1,0:T(8,128)(2,1)}, bf16[8,32,384]{2,1,0:T(8,128)(2,1)}, u32[]{:S(2)}, u32[]{:S(2)}) collective-permute-start(bf16[8,32,384]{2,1,0:T(8,128)(2,1)} %all_gather.9), channel_id=1, source_target_pairs={{0,4},{4,8},{8,12},{12,16},{16,20},{20,24},{24,28},{28,32},{32,36}... | collective-permute-start | bytes 589832 | tf_op jit(solution)/shard_map/ppermute | solution.py:16
  144.2 9.7 %collective-permute-start.3 = (bf16[8,32,384]{2,1,0:T(8,128)(2,1)S(1)}, bf16[8,32,384]{2,1,0:T(8,128)(2,1)S(1)}, u32[]{:S(2)}, u32[]{:S(2)}) collective-permute-start(bf16[8,32,384]{2,1,0:T(8,128)(2,1)S(1)} %all_gather.10), channel_id=1, source_target_pairs={{4,0},{8,4},{12,8},{16,12},{20,16},{24,20},{28,24},{32,28},{36,32}... | collective-permute-start | bytes 589832 | tf_op jit(solution)/shard_map/ppermute | solution.py:18
  148.4 13.6 %collective-permute-start.2 = (bf16[8,32,384]{2,1,0:T(8,128)(2,1)S(1)}, bf16[8,32,384]{2,1,0:T(8,128)(2,1)S(1)}, u32[]{:S(2)}, u32[]{:S(2)}) collective-permute-start(bf16[8,32,384]{2,1,0:T(8,128)(2,1)S(1)} %all_gather.10), channel_id=1, source_target_pairs={{0,4},{4,8},{8,12},{12,16},{16,20},{20,24},{24,28},{28,32},{32,36}... | collective-permute-start | bytes 589832 | tf_op jit(solution)/shard_map/ppermute | solution.py:16
  212.2 8.3 %collective-permute-start.7 = (bf16[8,32,256]{2,1,0:T(8,128)(2,1)S(1)}, bf16[8,32,256]{2,1,0:T(8,128)(2,1)S(1)}, u32[]{:S(2)}, u32[]{:S(2)}) collective-permute-start(bf16[8,32,256]{2,1,0:T(8,128)(2,1)S(1)} %all_gather.11), channel_id=1, source_target_pairs={{4,0},{8,4},{12,8},{16,12},{20,16},{24,20},{28,24},{32,28},{36,32}... | collective-permute-start | bytes 393224 | tf_op jit(solution)/shard_map/ppermute | solution.py:18
  214.5 12.2 %collective-permute-start.6 = (bf16[8,32,256]{2,1,0:T(8,128)(2,1)S(1)}, bf16[8,32,256]{2,1,0:T(8,128)(2,1)S(1)}, u32[]{:S(2)}, u32[]{:S(2)}) collective-permute-start(bf16[8,32,256]{2,1,0:T(8,128)(2,1)S(1)} %all_gather.11), channel_id=1, source_target_pairs={{0,4},{4,8},{8,12},{12,16},{16,20},{20,24},{24,28},{28,32},{32,36}... | collective-permute-start | bytes 393224 | tf_op jit(solution)/shard_map/ppermute | solution.py:16
  231.6 1.9 copy-start.3
